TPU v7x, 256 devices: a whole 4x4x8 slice. The times are simulated.
256 devices in a mesh: space: 32 (over y, z), spec: 8 (over x, core).
Axes of the slice: x: 4, y: 4, z: 8, core: 2. Of those that a mesh axis runs over, the one named last changes fastest.
Arguments:
- spectra: float32 [1296, 32768], P('spec', 'space'), may hold values from 0.1 to 2
- wet_mask: int32 [32768], P('space'), may hold values 0 or 1
- depth_class: int32 [32768], P('space'), may hold values from 0 to 31
- cg_table: float32 [36, 32], replicated, may hold values from 0.3 to 1
- neighbour: int32 [8, 32768], P(None, 'space'), may hold values from 0 to 3071, as said below
- edge_weight: float32 [8, 32768], P(None, 'space'), may hold values from 0.02 to 0.11
- edge_angle: float32 [8, 32768], P(None, 'space'), may hold values from -3.140625 to 3.140625
- send_list: int32 [32, 32, 64], P('space'), may hold values from 0 to 1023, as said below
- friction: float32 [32768], P('space'), may hold values from 0.2 to 1.5
- wind_dir: float32 [32768], P('space'), may hold values from -3.140625 to 3.140625
Outputs:
- spectra_next: float32 [1296, 32768], P('spec', 'space')
- energy: float32 [32768], P(('space', 'spec'))
Inputs may be any that keep to these rules, and one draw needn't show every extreme that they name: `send_list`: block s sends only to blocks (s + 1), (s - 1), (s + 2), (s - 2) and (s + 16), all modulo 32; entries of any other pair, and entries at or past a pair's used count, are 0. The pair from each block s to block (s + 1) % 32 uses all 64 slots and its slot 0 holds node 1023. `neighbour`: A ghost entry 1024 + p * 64 + g has p among the blocks that send to the node's block and g below the count that block p uses towards it; an unused slot holds the node's own local index. Node 0 of every block b has slot 0 at ghost slot 63 from block (b - 1) % 32.
All inputs are finite; a program needn't handle non-finite values. No bound on the sum of `wet_mask` on one device may be relied on, other than what follows from the above.
Results may differ from a plain program's by a relative error of at most 0.000067.
Values sent between devices are 32-bit elements; how exact they have to be, the bound alone decides.
No kernel may reach another device: no remote copies, remote signals or barrier semaphores. Data moves between devices by JAX's collectives and lax.ppermute only.
A program may use at most 64 MiB of HBM per device.

v0:
```python
import math
import jax
import jax.numpy as jnp
from jax import lax
from jax.sharding import PartitionSpec as P

NDIR = 36
NFREQ = 36
NCLASS = 32


def spectral_constants():
    level_index = jnp.arange(NFREQ, dtype=jnp.float32)
    frequency = 0.04 * jnp.exp(level_index * jnp.float32(math.log(1.1)))
    spread = 0.1 * frequency
    band_weight = spread / (NDIR * jnp.sum(spread))
    direction_angle = jnp.arange(NDIR, dtype=jnp.float32) * jnp.float32(2.0 * math.pi / NDIR)
    return (frequency, band_weight, jnp.cos(direction_angle), jnp.sin(direction_angle))


def point_source(values, energy, moment, freq_col, cos_col, sin_col, friction_row, dir_row):
    top_freq = 0.04 * jnp.exp(jnp.float32(NFREQ - 1) * jnp.float32(math.log(1.1)))
    mean_freq = (moment + 4e-08) / (energy + 1e-06)
    steepness = energy * (mean_freq / 0.8) ** 4
    dissipation = (steepness**2)[None, :] * freq_col[:, None] / mean_freq[None, :]
    drive = (
        cos_col[:, None] * jnp.cos(dir_row)[None, :] + sin_col[:, None] * jnp.sin(dir_row)[None, :]
    )
    relative = freq_col / top_freq
    wind_input = 0.5 * jnp.maximum(
        4.0 * friction_row[None, :] * relative[:, None] * drive - 1.0, 0.0
    )
    return values * jnp.exp(0.25 * (wind_input - dissipation))


def per_device(
    spectra,
    wet_mask,
    depth_class,
    cg_table,
    neighbour,
    edge_weight,
    edge_angle,
    send_list,
    friction,
    wind_dir,
):
    comp_count, node_count = spectra.shape
    spec_count = lax.axis_size("spec")
    slot_count = neighbour.shape[0]
    frequency, band_weight, dir_cosine, dir_sine = spectral_constants()
    comp_range = lax.axis_index("spec") * comp_count + jnp.arange(comp_count, dtype=jnp.int32)
    freq_index = comp_range // NDIR
    dir_index = comp_range % NDIR
    cos_col = dir_cosine[dir_index]
    sin_col = dir_sine[dir_index]
    wet_float = wet_mask.astype(jnp.float32)
    masked = spectra * wet_float[None, :]
    outgoing = jnp.take(masked, send_list[0].reshape(-1), axis=1)
    ghost_values = lax.all_to_all(outgoing, "space", split_axis=1, concat_axis=1, tiled=True)
    class_hits = (jnp.arange(NCLASS, dtype=jnp.int32)[:, None] == depth_class[None, :]).astype(
        jnp.float32
    )
    group_speed = jnp.dot(
        cg_table[freq_index],
        class_hits,
        precision=lax.Precision.HIGHEST,
        preferred_element_type=jnp.float32,
    )
    accumulated = jnp.zeros_like(masked)
    extended = jnp.concatenate([masked, ghost_values], axis=1)
    gathered_all = jnp.take(extended, neighbour.reshape(-1), axis=1)
    for slot_index in range(slot_count):
        gathered = gathered_all[:, slot_index * node_count : (slot_index + 1) * node_count]
        alignment = (
            cos_col[:, None] * jnp.cos(edge_angle[slot_index])[None, :]
            + sin_col[:, None] * jnp.sin(edge_angle[slot_index])[None, :]
        )
        accumulated = accumulated + group_speed * edge_weight[slot_index][None, :] * jnp.maximum(
            alignment, 0.0
        ) * (gathered - masked)
    advected = (masked + accumulated) * wet_float[None, :]
    point_count = node_count // spec_count
    offset = lax.axis_index("spec") * point_count
    blocked = advected.reshape(comp_count, spec_count, point_count)
    gathered_points = lax.all_to_all(
        blocked, "spec", split_axis=1, concat_axis=0, tiled=True
    ).reshape(comp_count * spec_count, point_count)
    full_range = jnp.arange(comp_count * spec_count, dtype=jnp.int32)
    full_freq = full_range // NDIR
    full_dir = full_range % NDIR
    freq_col = frequency[full_freq]
    weight_col = band_weight[full_freq]
    energy = jnp.sum(gathered_points * weight_col[:, None], axis=0)
    moment = jnp.sum(gathered_points * (weight_col * freq_col)[:, None], axis=0)
    friction_part = lax.dynamic_slice_in_dim(friction, offset, point_count)
    wind_part = lax.dynamic_slice_in_dim(wind_dir, offset, point_count)
    updated = point_source(
        gathered_points,
        energy,
        moment,
        freq_col,
        dir_cosine[full_dir],
        dir_sine[full_dir],
        friction_part,
        wind_part,
    )
    returned = lax.all_to_all(
        updated.reshape(comp_count * spec_count, 1, point_count),
        "spec",
        split_axis=0,
        concat_axis=1,
        tiled=True,
    )
    return (returned.reshape(comp_count, node_count), energy)


def solution(mesh):
    placed = (
        P("spec", "space"),
        P("space"),
        P("space"),
        P(),
        P(None, "space"),
        P(None, "space"),
        P(None, "space"),
        P("space", None, None),
        P("space"),
        P("space"),
    )
    return jax.shard_map(
        per_device,
        mesh=mesh,
        in_specs=placed,
        out_specs=(P("spec", "space"), P(("space", "spec"))),
        check_vma=False,
    )
```

profile of v0, /device:TPU:1, one launch (start us, length us, event | category | flops | bytes accessed | tf_op | source)
XLA Modules:
  0.0 211.6 jit_solution(6362153186703250153)
XLA Ops:
  0.6 0.8 reshape_squeeze.6
  1.4 0.7 compare_and_fusion.1
  2.2 0.7 convert_element_type.4
  2.8 1.2 broadcast_multiply_fusion
  4.0 0.3 copy.29
  4.4 6.6 %gather_fusion.3 = f32[2048,162]{1,0:T(8,128)S(1)} fusion(f32[162,1024]{0,1:T(8,128)S(1)} %copy.29, s32[2048]{0:T(1024)S(1)} %broadcast_clamp_fusion.1), kind=kCustom, calls=%fused_computation.3 | custom fusion | bytes 2662400 | tf_op jit(solution)/shard_map/jit(_take)/gather | solution.py:59
  11.0 1.7 broadcast_select_fusion
  12.7 12.2 %all-to-all-start = ((f32[162,32,64]{0,2,1:T(8,128)}), f32[162,32,64]{0,2,1:T(8,128)S(1)}, u32[]{:S(2)}, u32[]{:S(2)}) async-start(f32[162,32,64]{0,2,1:T(8,128)} %broadcast_select_fusion), calls=%async_computation | async-start | bytes 4194304 | tf_op jit(solution)/shard_map/all_to_all | solution.py:60
  26.8 0.6 fusion.27
  28.1 0.7 fusion.36
  28.8 0.7 fusion.35
  29.6 0.7 fusion.34
  30.3 0.7 fusion.33
  31.0 0.1 compare_reduce_fusion
  31.1 0.1 compare_reduce_fusion.1
  31.2 0.1 compare_reduce_fusion.2
  31.2 0.1 compare_reduce_fusion.3
  31.3 0.1 compare_reduce_fusion.4
  31.4 0.1 compare_reduce_fusion.5
  31.5 0.1 compare_reduce_fusion.6
  31.5 0.1 compare_reduce_fusion.7
  31.6 0.1 compare_reduce_fusion.8
  31.7 0.1 compare_reduce_fusion.9
  31.9 0.1 compare_reduce_fusion.12
  32.1 0.1 compare_reduce_fusion.15
  32.2 0.1 compare_reduce_fusion.17
  32.4 0.1 compare_reduce_fusion.20
  32.7 0.1 compare_reduce_fusion.23
  33.0 0.7 fusion.32
  33.7 0.7 fusion.31
  34.5 1.6 gather_fusion.2
  36.1 1.6 gather_fusion.1
  37.6 0.7 fusion.30
  38.4 0.1 copy.27
  38.5 0.7 gather_fusion
  39.2 0.8 dynamic-slice_cosine_fusion
  40.0 4.5 %fusion.18 = f32[1296]{0:T(1024)S(1)} fusion(f32[]{:T(128)} %bitcast.173, f32[]{:T(128)} %bitcast.174, f32[]{:T(128)} %bitcast.175, f32[]{:T(128)} %bitcast.176, f32[]{:T(128)} %bitcast.177, f32[]{:T(128)} %bitcast.179, f32[]{:T(128)} %bitcast.178), kind=kLoop, calls=%fused_computation.142 | loop fusion | flops 29808 | bytes 5212 | tf_op jit(solution)/shard_map/gather | solution.py:93
  44.5 4.3 %fusion.19 = f32[1296]{0:T(1024)S(1)} fusion(f32[]{:T(128)} %bitcast.64, f32[]{:T(128)} %bitcast.65, f32[]{:T(128)} %bitcast.66, f32[]{:T(128)} %bitcast.67, f32[]{:T(128)} %bitcast.68, f32[]{:T(128)} %bitcast.70, f32[]{:T(128)} %bitcast.69), kind=kLoop, calls=%fused_computation.143 | loop fusion | flops 29808 | bytes 5212 | tf_op jit(solution)/shard_map/gather | solution.py:92
  48.8 4.3 %fusion.20 = f32[1296]{0:T(1024)S(1)} fusion(f32[]{:T(128)} %bitcast.136, f32[]{:T(128)} %bitcast.137, f32[]{:T(128)} %bitcast.138, f32[]{:T(128)} %bitcast.139, f32[]{:T(128)} %bitcast.140, f32[]{:T(128)} %bitcast.142, f32[]{:T(128)} %bitcast.141), kind=kLoop, calls=%fused_computation.144 | loop fusion | flops 27216 | bytes 5212 | tf_op jit(solution)/shard_map/gather | solution.py:104
  53.2 17.8 %select_select_fusion = f32[1296]{0:T(1024)S(1)} fusion(pred[1296]{0:T(1024)(128)(4,1)S(1)} %compare_reduce_fusion.29, pred[1296]{0:T(1024)(128)(4,1)S(1)} %compare_reduce_fusion.30, pred[1296]{0:T(1024)(128)(4,1)S(1)} %compare_reduce_fusion.31, pred[1296]{0:T(1024)(128)(4,1)S(1)} %compare_reduce_fusion.32, pred[1296]{0:T(1024)(128)(4,1)S(1)} %compare_reduce_fusion.33, ...), kind=kLoop, calls=%fused_computation.136 | loop fusion | flops 37584 | bytes 48068 | tf_op jit(solution)/shard_map/gather | solution.py:93
  71.1 18.0 %broadcast_multiply_fusion.1 = (f32[1296]{0:T(1024)S(1)}, f32[1296]{0:T(1024)S(1)}) fusion(pred[1296]{0:T(1024)(128)(4,1)S(1)} %compare_reduce_fusion.29, pred[1296]{0:T(1024)(128)(4,1)S(1)} %compare_reduce_fusion.30, pred[1296]{0:T(1024)(128)(4,1)S(1)} %compare_reduce_fusion.31, pred[1296]{0:T(1024)(128)(4,1)S(1)} %compare_reduce_fusion.32, ...), kind=kLoop, calls=%fused_computation.149 | loop fusion | flops 38880 | bytes 53252 | tf_op jit(solution)/shard_map/div | solution.py:29
  89.1 1.0 slice_cosine_fusion.7
  90.1 1.3 copy-done.1
  91.5 2.1 pad_maximum_fusion
  93.5 31.4 %gather_fusion.4 = f32[8192,162]{1,0:T(8,128)} fusion(f32[162,3072]{0,1:T(8,128)S(1)} %pad_maximum_fusion, s32[8192]{0:T(1024)S(1)} %broadcast_clamp_fusion), kind=kCustom, calls=%fused_computation.4 | custom fusion | bytes 10649600 | tf_op jit(solution)/shard_map/jit(_take)/gather | solution.py:72
  124.9 8.4 %copy.30 = f32[8192,162]{0,1:T(8,128)} copy(f32[8192,162]{1,0:T(8,128)} %gather_fusion.4) | data formatting | bytes 10616832 | tf_op jit(solution)/shard_map/jit(_take)/gather | solution.py:72
  133.3 3.1 %select_bitcast_fusion = f32[162,8192]{1,0:T(8,128)S(1)} fusion(f32[8192,162]{0,1:T(8,128)} %copy.30, pred[8192]{0:T(1024)(128)(4,1)S(1)} %compare_and_fusion), kind=kLoop, calls=%fused_computation.5 | loop fusion | flops 1327104 | bytes 10625024 | tf_op jit(solution)/shard_map/jit(_take)/select_n | solution.py:72
  136.4 2.4 %fusion.3 = f32[162,1024]{1,0:T(8,128)S(1)} fusion(f32[162,8192]{1,0:T(8,128)S(1)} %select_bitcast_fusion, f32[162,32]{1,0:T(8,128)S(1)} %gather_fusion, f32[1024]{0:T(1024)S(1)} %bitcast.243, f32[1024]{0:T(1024)S(1)} %bitcast.249, f32[1024]{0:T(1024)S(1)} %bitcast.233, f32[1024]{0:T(1024)S(1)} %bitcast.242, f32[1024]{0:T(1024)S(1)} %bitcast.250, ...), kind=kOutput, calls=%fused_computation.12 | convolution fusion | flops 76009472 | bytes 6764048 | tf_op jit(solution)/shard_map/dot_general | solution.py:64
  138.8 0.1 copy.39
  139.0 1.0 copy.31
  140.0 5.2 %all-to-all-start.1 = ((f32[162,8,128]{2,0,1:T(8,128)}), f32[162,8,128]{2,0,1:T(8,128)S(1)}, u32[]{:S(2)}, u32[]{:S(2)}) async-start(f32[162,8,128]{2,0,1:T(8,128)} %copy.31), calls=%async_computation.1 | async-start | bytes 1376256 | tf_op jit(solution)/shard_map/all_to_all | solution.py:86
  145.3 0.1 mul.694
  145.4 0.1 gather.43
  145.5 4.6 %fusion.21 = f32[1296]{0:T(1024)S(1)} fusion(f32[]{:T(128)} %bitcast.100, f32[]{:T(128)} %bitcast.101, f32[]{:T(128)} %bitcast.102, f32[]{:T(128)} %bitcast.103, f32[]{:T(128)} %bitcast.104, f32[]{:T(128)} %bitcast.106, f32[]{:T(128)} %bitcast.105), kind=kLoop, calls=%fused_computation.145 | loop fusion | flops 27216 | bytes 5212 | tf_op jit(solution)/shard_map/gather | solution.py:103
  150.0 0.7 fusion.29
  150.8 18.1 %select_select_fusion.1 = f32[1296]{0:T(1024)S(1)} fusion(pred[1296]{0:T(1024)(128)(4,1)S(1)} %compare_reduce_fusion, pred[1296]{0:T(1024)(128)(4,1)S(1)} %compare_reduce_fusion.1, pred[1296]{0:T(1024)(128)(4,1)S(1)} %compare_reduce_fusion.2, pred[1296]{0:T(1024)(128)(4,1)S(1)} %compare_reduce_fusion.3, pred[1296]{0:T(1024)(128)(4,1)S(1)} %compare_reduce_fusion.4, ...), kind=kLoop, calls=%fused_computation.137 | loop fusion | flops 37584 | bytes 48068 | tf_op jit(solution)/shard_map/gather | solution.py:104
  168.9 18.2 %select_select_fusion.2 = f32[1296]{0:T(1024)S(1)} fusion(pred[1296]{0:T(1024)(128)(4,1)S(1)} %compare_reduce_fusion, pred[1296]{0:T(1024)(128)(4,1)S(1)} %compare_reduce_fusion.1, pred[1296]{0:T(1024)(128)(4,1)S(1)} %compare_reduce_fusion.2, pred[1296]{0:T(1024)(128)(4,1)S(1)} %compare_reduce_fusion.3, pred[1296]{0:T(1024)(128)(4,1)S(1)} %compare_reduce_fusion.4, ...), kind=kLoop, calls=%fused_computation.138 | loop fusion | flops 37584 | bytes 48068 | tf_op jit(solution)/shard_map/gather | solution.py:103
  187.2 0.4 multiply_reduce_fusion
  187.6 1.1 exponential_multiply_fusion
  188.7 15.6 %all_to_all.39 = f32[1296,1,128]{2,1,0:T(1,128)S(1)} all-to-all(f32[1296,1,128]{2,1,0:T(1,128)S(1)} %bitcast.218), channel_id=1, replica_groups=mesh['space'=32,'spec'=8] {'spec'}, dimensions={0} | all-to-all | bytes 1327104 | tf_op jit(solution)/shard_map/all_to_all | solution.py:108
  204.4 0.5 broadcast.1224
  204.9 5.5 %reduce.129 = f32[1296,128]{1,0:T(8,128)S(1)} reduce(f32[1296,1,128]{2,1,0:T(1,128)S(1)} %all_to_all.39, f32[]{:T(128)} %broadcast.1224), dimensions={1}, to_apply=%all_to_all.33.reduce_sub_computation.3 | reduce | bytes 1327108 | tf_op jit(solution)/shard_map/all_to_all | solution.py:108
  210.4 0.1 copy.46
  210.6 1.0 copy.40
  (82 shorter events, 3.3 us)
Async XLA Ops:
  4.3 6.7 %copy-start = (f32[162,1024]{0,1:T(8,128)}, f32[162,1024]{0,1:T(8,128)S(1)}, u32[]{:S(2)}) copy-start(f32[162,1024]{0,1:T(8,128)S(1)} %copy.29) | copy-start | bytes 1990660
  12.7 25.6 %copy-start.3 = (s32[8,1024]{1,0:T(8,128)S(1)}, s32[8,1024]{1,0:T(8,128)}, u32[]{:S(2)}) copy-start(s32[8,1024]{1,0:T(8,128)} %param.14) | copy-start | bytes 98308
  12.7 25.7 %copy-start.6 = (f32[36,32]{0,1:T(8,128)S(1)}, f32[36,32]{0,1:T(8,128)}, u32[]{:S(2)}) copy-start(f32[36,32]{0,1:T(8,128)} %param.13) | copy-start | bytes 13828
  12.7 40.5 %copy-start.5 = (f32[8,1024]{1,0:T(8,128)S(1)}, f32[8,1024]{1,0:T(8,128)}, u32[]{:S(2)}) copy-start(f32[8,1024]{1,0:T(8,128)} %param.15) | copy-start | bytes 98308
  12.7 76.3 %copy-start.4 = (f32[8,1024]{1,0:T(8,128)S(1)}, f32[8,1024]{1,0:T(8,128)}, u32[]{:S(2)}) copy-start(f32[8,1024]{1,0:T(8,128)} %param.16) | copy-start | bytes 98308
  12.7 77.4 %all-to-all-start = ((f32[162,32,64]{0,2,1:T(8,128)}), f32[162,32,64]{0,2,1:T(8,128)S(1)}, u32[]{:S(2)}, u32[]{:S(2)}) async-start(f32[162,32,64]{0,2,1:T(8,128)} %broadcast_select_fusion), calls=%async_computation | async-start | bytes 4194304 | tf_op jit(solution)/shard_map/all_to_all | solution.py:60
  90.1 1.4 copy-start.1
  133.3 3.1 %copy-start.2 = (f32[162,1024]{1,0:T(8,128)S(1)}, f32[162,1024]{1,0:T(8,128)}, u32[]{:S(2)}) copy-start(f32[162,1024]{1,0:T(8,128)} %param.10) | copy-start | bytes 1990660
  133.3 3.1 %copy-start.8 = (s32[1024]{0:T(1024)S(1)}, s32[1024]{0:T(1024)}, u32[]{:S(2)}) copy-start(s32[1024]{0:T(1024)} %param.12) | copy-start | bytes 12292
  140.0 47.2 %all-to-all-start.1 = ((f32[162,8,128]{2,0,1:T(8,128)}), f32[162,8,128]{2,0,1:T(8,128)S(1)}, u32[]{:S(2)}, u32[]{:S(2)}) async-start(f32[162,8,128]{2,0,1:T(8,128)} %copy.31), calls=%async_computation.1 | async-start | bytes 1376256 | tf_op jit(solution)/shard_map/all_to_all | solution.py:86
  187.6 22.9 %copy-start.7 = (f32[128]{0:T(128)}, f32[128]{0:T(128)S(1)}, u32[]{:S(2)}) copy-start(f32[128]{0:T(128)S(1)} %get-tuple-element.3) | copy-start | bytes 1540
where the time goes:
time: 214 us; the launch traced here: 212 us
  other arithmetic  112 us (52%)
  local copies, waits for them, and re-layouts  62.7 us (29%)
  starting transfers between devices  17.4 us (8%)
  blocking collectives  15.6 us (7%)
  matrix products  2.4 us (1%)
    gather x2, local copies, waits for them, and re-layouts, per_device(): gathered_all = jnp.take(extended, neighbour.reshape(-1), axis=1)  39.8 us
    gather x31, other arithmetic, per_device(): dir_cosine[full_dir]  24.8 us
    gather x2, other arithmetic, per_device(): dir_sine[full_dir]  22.4 us
    gather x2, other arithmetic, per_device(): weight_col = band_weight[full_freq]  22.3 us
    div x1, other arithmetic, point_source(): relative = freq_col / top_freq  18 us
    all_to_all x1, blocking collectives, per_device(): lax.all_to_all(updated.reshape(comp_count * spec_count, 1, point_count),...  15.6 us
    all_to_all x1, starting transfers between devices, per_device(): lax.all_to_all(outgoing, 'space', split_axis=1, concat_axis=1, tiled=True)  12.2 us
    gather x1, local copies, waits for them, and re-layouts, per_device(): outgoing = jnp.take(masked, send_list[0].reshape(-1), axis=1)  6.64 us
  transfers between devices with their start and end apart: 2, of which 0 were waited for; matrix products, arithmetic and copies ran while one was open for 50% of the time, Pallas kernels for 0%

commit v1 on v0

--- a/solution.py
+++ b/solution.py
@@ -57,7 +57,12 @@
     wet_float = wet_mask.astype(jnp.float32)
     masked = spectra * wet_float[None, :]
     outgoing = jnp.take(masked, send_list[0].reshape(-1), axis=1)
-    ghost_values = lax.all_to_all(outgoing, "space", split_axis=1, concat_axis=1, tiled=True)
+    ghost_values = jnp.concatenate(
+        lax.all_to_all(
+            jnp.stack(jnp.split(outgoing, lax.axis_size("space"), axis=1)), "space", 0, 0
+        ),
+        axis=1,
+    )
     class_hits = (jnp.arange(NCLASS, dtype=jnp.int32)[:, None] == depth_class[None, :]).astype(
         jnp.float32
     )

time: 214 us -> 232 us (1.084)
  local copies, waits for them, and re-layouts: 62.7 us -> 83.4 us
    unnamed x23 -> x54, local copies, waits for them, and re-layouts: 2.64 us -> 22 us
  transfers between devices with their start and end apart: 2 -> 2, of which waited for: 0 -> 0; matrix products, arithmetic and copies ran while one was open for 50% -> 46% of each run, Pallas kernels for 0% -> 0%
where the time goes in v1:
time: 232 us; the launch traced here: 230 us
  other arithmetic  110 us (47%)
  local copies, waits for them, and re-layouts  83.4 us (36%)
  starting transfers between devices  17.5 us (8%)
  blocking collectives  15.6 us (7%)
  matrix products  2.4 us (1%)
    gather x2, local copies, waits for them, and re-layouts, per_device(): gathered_all = jnp.take(extended, neighbour.reshape(-1), axis=1)  39.8 us
    gather x31, other arithmetic, per_device(): dir_cosine[full_dir]  24.8 us
    gather x2, other arithmetic, per_device(): dir_sine[full_dir]  22.4 us
    gather x2, other arithmetic, per_device(): weight_col = band_weight[full_freq]  22.3 us
    unnamed x54, local copies, waits for them, and re-layouts  22 us
    div x1, other arithmetic, point_source(): relative = freq_col / top_freq  18 us
    all_to_all x1, blocking collectives, per_device(): lax.all_to_all(updated.reshape(comp_count * spec_count, 1, point_count),...  15.6 us
    all_to_all x1, starting transfers between devices, per_device(): lax.all_to_all(jnp.stack(jnp.split(outgoing, lax.axis_size('space'), axis...  12 us
  transfers between devices with their start and end apart: 2, of which 0 were waited for; matrix products, arithmetic and copies ran while one was open for 46% of the time, Pallas kernels for 0%

profile of v1, /device:TPU:1, one launch (start us, length us, event | category | flops | bytes accessed | tf_op | source)
XLA Modules:
  0.0 230.3 jit_solution(17810889938215656402)
XLA Ops:
  0.6 0.8 reshape_squeeze.6
  1.4 0.8 reshape_squeeze.5
  2.2 0.7 convert_element_type.4
  2.9 1.2 broadcast_multiply_fusion
  4.5 6.6 %gather_fusion.3 = f32[2048,162]{1,0:T(8,128)S(1)} fusion(f32[162,1024]{0,1:T(8,128)S(1)} %copy.29, s32[2048]{0:T(1024)S(1)} %broadcast_clamp_fusion.1), kind=kCustom, calls=%fused_computation.3 | custom fusion | bytes 2662400 | tf_op jit(solution)/shard_map/jit(_take)/gather | solution.py:59
  11.5 0.6 fusion.48
  12.1 0.6 fusion.47
  12.7 0.6 fusion.46
  13.3 0.6 fusion.45
  14.6 0.6 fusion.43
  15.2 0.6 fusion.42
  16.5 0.6 fusion.40
  17.1 0.6 fusion.39
  17.7 0.6 fusion.38
  19.6 0.6 fusion.35
  20.2 0.6 fusion.34
  20.8 0.6 fusion.33
  21.5 0.6 fusion.32
  22.7 0.6 fusion.30
  24.6 0.6 fusion.27
  25.2 0.6 fusion.26
  25.8 0.6 fusion.25
  26.4 0.6 fusion.24
  27.0 0.6 fusion.23
  28.3 0.6 fusion.21
  28.9 0.6 fusion.20
  29.5 0.6 fusion.19
  30.2 0.6 fusion.18
  30.8 0.6 fusion.17
  31.4 12.0 %all-to-all-start = ((f32[32,162,64]{1,2,0:T(8,128)}), f32[32,162,64]{1,2,0:T(8,128)S(1)}, u32[]{:S(2)}, u32[]{:S(2)}) async-start(f32[32,162,64]{1,2,0:T(8,128)} %fusion.17), calls=%async_computation | async-start | bytes 4194304 | tf_op jit(solution)/shard_map/all_to_all | solution.py:61
  43.6 0.6 fusion.59
  44.9 0.7 fusion.68
  45.7 0.7 fusion.67
  48.2 0.7 fusion.66
  48.9 0.7 fusion.65
  49.6 0.7 fusion.64
  50.4 0.7 fusion.63
  53.1 1.6 gather_fusion.2
  54.6 1.6 gather_fusion.1
  56.2 0.7 fusion.62
  57.1 0.7 gather_fusion
  57.8 0.8 dynamic-slice_cosine_fusion
  58.6 4.5 %fusion.50 = f32[1296]{0:T(1024)S(1)} fusion(f32[]{:T(128)} %bitcast.204, f32[]{:T(128)} %bitcast.205, f32[]{:T(128)} %bitcast.206, f32[]{:T(128)} %bitcast.207, f32[]{:T(128)} %bitcast.208, f32[]{:T(128)} %bitcast.210, f32[]{:T(128)} %bitcast.209), kind=kLoop, calls=%fused_computation.206 | loop fusion | flops 29808 | bytes 5212 | tf_op jit(solution)/shard_map/gather | solution.py:98
  63.1 4.3 %fusion.51 = f32[1296]{0:T(1024)S(1)} fusion(f32[]{:T(128)} %bitcast.95, f32[]{:T(128)} %bitcast.96, f32[]{:T(128)} %bitcast.97, f32[]{:T(128)} %bitcast.98, f32[]{:T(128)} %bitcast.99, f32[]{:T(128)} %bitcast.101, f32[]{:T(128)} %bitcast.100), kind=kLoop, calls=%fused_computation.207 | loop fusion | flops 29808 | bytes 5212 | tf_op jit(solution)/shard_map/gather | solution.py:97
  67.4 4.3 %fusion.52 = f32[1296]{0:T(1024)S(1)} fusion(f32[]{:T(128)} %bitcast.167, f32[]{:T(128)} %bitcast.168, f32[]{:T(128)} %bitcast.169, f32[]{:T(128)} %bitcast.170, f32[]{:T(128)} %bitcast.171, f32[]{:T(128)} %bitcast.173, f32[]{:T(128)} %bitcast.172), kind=kLoop, calls=%fused_computation.208 | loop fusion | flops 27216 | bytes 5212 | tf_op jit(solution)/shard_map/gather | solution.py:109
  71.8 17.8 %select_select_fusion = f32[1296]{0:T(1024)S(1)} fusion(pred[1296]{0:T(1024)(128)(4,1)S(1)} %compare_reduce_fusion.29, pred[1296]{0:T(1024)(128)(4,1)S(1)} %compare_reduce_fusion.30, pred[1296]{0:T(1024)(128)(4,1)S(1)} %compare_reduce_fusion.31, pred[1296]{0:T(1024)(128)(4,1)S(1)} %compare_reduce_fusion.32, pred[1296]{0:T(1024)(128)(4,1)S(1)} %compare_reduce_fusion.33, ...), kind=kLoop, calls=%fused_computation.199 | loop fusion | flops 37584 | bytes 48068 | tf_op jit(solution)/shard_map/gather | solution.py:98
  89.7 18.0 %broadcast_multiply_fusion.1 = (f32[1296]{0:T(1024)S(1)}, f32[1296]{0:T(1024)S(1)}) fusion(pred[1296]{0:T(1024)(128)(4,1)S(1)} %compare_reduce_fusion.29, pred[1296]{0:T(1024)(128)(4,1)S(1)} %compare_reduce_fusion.30, pred[1296]{0:T(1024)(128)(4,1)S(1)} %compare_reduce_fusion.31, pred[1296]{0:T(1024)(128)(4,1)S(1)} %compare_reduce_fusion.32, ...), kind=kLoop, calls=%fused_computation.213 | loop fusion | flops 38880 | bytes 53252 | tf_op jit(solution)/shard_map/div | solution.py:29
  107.7 1.0 slice_cosine_fusion.7
  108.7 1.3 copy-done.1
  110.0 2.1 pad_maximum_fusion
  112.1 31.4 %gather_fusion.4 = f32[8192,162]{1,0:T(8,128)} fusion(f32[162,3072]{0,1:T(8,128)S(1)} %pad_maximum_fusion, s32[8192]{0:T(1024)S(1)} %broadcast_clamp_fusion), kind=kCustom, calls=%fused_computation.4 | custom fusion | bytes 10649600 | tf_op jit(solution)/shard_map/jit(_take)/gather | solution.py:77
  143.5 8.4 %copy.30 = f32[8192,162]{0,1:T(8,128)} copy(f32[8192,162]{1,0:T(8,128)} %gather_fusion.4) | data formatting | bytes 10616832 | tf_op jit(solution)/shard_map/jit(_take)/gather | solution.py:77
  151.9 3.1 %select_bitcast_fusion = f32[162,8192]{1,0:T(8,128)S(1)} fusion(f32[8192,162]{0,1:T(8,128)} %copy.30, pred[8192]{0:T(1024)(128)(4,1)S(1)} %compare_and_fusion), kind=kLoop, calls=%fused_computation.5 | loop fusion | flops 1327104 | bytes 10625024 | tf_op jit(solution)/shard_map/jit(_take)/select_n | solution.py:77
  155.0 2.4 %fusion.3 = f32[162,1024]{1,0:T(8,128)S(1)} fusion(f32[162,8192]{1,0:T(8,128)S(1)} %select_bitcast_fusion, f32[162,32]{1,0:T(8,128)S(1)} %gather_fusion, f32[1024]{0:T(1024)S(1)} %bitcast.367, f32[1024]{0:T(1024)S(1)} %bitcast.373, f32[1024]{0:T(1024)S(1)} %bitcast.357, f32[1024]{0:T(1024)S(1)} %bitcast.366, f32[1024]{0:T(1024)S(1)} %bitcast.374, ...), kind=kOutput, calls=%fused_computation.12 | convolution fusion | flops 76009472 | bytes 6764048 | tf_op jit(solution)/shard_map/dot_general | solution.py:69
  157.6 1.0 copy.31
  158.6 5.4 %all-to-all-start.1 = ((f32[162,8,128]{2,0,1:T(8,128)}), f32[162,8,128]{2,0,1:T(8,128)S(1)}, u32[]{:S(2)}, u32[]{:S(2)}) async-start(f32[162,8,128]{2,0,1:T(8,128)} %copy.31), calls=%async_computation.1 | async-start | bytes 1376256 | tf_op jit(solution)/shard_map/all_to_all | solution.py:91
  164.2 4.6 %fusion.53 = f32[1296]{0:T(1024)S(1)} fusion(f32[]{:T(128)} %bitcast.131, f32[]{:T(128)} %bitcast.132, f32[]{:T(128)} %bitcast.133, f32[]{:T(128)} %bitcast.134, f32[]{:T(128)} %bitcast.135, f32[]{:T(128)} %bitcast.137, f32[]{:T(128)} %bitcast.136), kind=kLoop, calls=%fused_computation.209 | loop fusion | flops 27216 | bytes 5212 | tf_op jit(solution)/shard_map/gather | solution.py:108
  168.8 0.7 fusion.61
  169.5 18.1 %select_select_fusion.1 = f32[1296]{0:T(1024)S(1)} fusion(pred[1296]{0:T(1024)(128)(4,1)S(1)} %compare_reduce_fusion, pred[1296]{0:T(1024)(128)(4,1)S(1)} %compare_reduce_fusion.1, pred[1296]{0:T(1024)(128)(4,1)S(1)} %compare_reduce_fusion.2, pred[1296]{0:T(1024)(128)(4,1)S(1)} %compare_reduce_fusion.3, pred[1296]{0:T(1024)(128)(4,1)S(1)} %compare_reduce_fusion.4, ...), kind=kLoop, calls=%fused_computation.200 | loop fusion | flops 37584 | bytes 48068 | tf_op jit(solution)/shard_map/gather | solution.py:109
  187.6 18.2 %select_select_fusion.2 = f32[1296]{0:T(1024)S(1)} fusion(pred[1296]{0:T(1024)(128)(4,1)S(1)} %compare_reduce_fusion, pred[1296]{0:T(1024)(128)(4,1)S(1)} %compare_reduce_fusion.1, pred[1296]{0:T(1024)(128)(4,1)S(1)} %compare_reduce_fusion.2, pred[1296]{0:T(1024)(128)(4,1)S(1)} %compare_reduce_fusion.3, pred[1296]{0:T(1024)(128)(4,1)S(1)} %compare_reduce_fusion.4, ...), kind=kLoop, calls=%fused_computation.201 | loop fusion | flops 37584 | bytes 48068 | tf_op jit(solution)/shard_map/gather | solution.py:108
  206.4 1.1 exponential_multiply_fusion
  207.5 15.6 %all_to_all.35 = f32[1296,1,128]{2,1,0:T(1,128)S(1)} all-to-all(f32[1296,1,128]{2,1,0:T(1,128)S(1)} %bitcast.342), channel_id=1, replica_groups=mesh['space'=32,'spec'=8] {'spec'}, dimensions={0} | all-to-all | bytes 1327104 | tf_op jit(solution)/shard_map/all_to_all | solution.py:113
  223.6 5.5 %reduce.129 = f32[1296,128]{1,0:T(8,128)S(1)} reduce(f32[1296,1,128]{2,1,0:T(1,128)S(1)} %all_to_all.35, f32[]{:T(128)} %broadcast.1222), dimensions={1}, to_apply=%all_to_all.29.reduce_sub_computation.3 | reduce | bytes 1327108 | tf_op jit(solution)/shard_map/all_to_all | solution.py:113
  229.4 1.0 copy.40
  (115 shorter events, 11.4 us)
Async XLA Ops:
  4.4 6.7 %copy-start = (f32[162,1024]{0,1:T(8,128)}, f32[162,1024]{0,1:T(8,128)S(1)}, u32[]{:S(2)}) copy-start(f32[162,1024]{0,1:T(8,128)S(1)} %copy.29) | copy-start | bytes 1990660
  31.4 77.3 %all-to-all-start = ((f32[32,162,64]{1,2,0:T(8,128)}), f32[32,162,64]{1,2,0:T(8,128)S(1)}, u32[]{:S(2)}, u32[]{:S(2)}) async-start(f32[32,162,64]{1,2,0:T(8,128)} %fusion.17), calls=%async_computation | async-start | bytes 4194304 | tf_op jit(solution)/shard_map/all_to_all | solution.py:61
  43.5 13.5 %copy-start.3 = (s32[8,1024]{1,0:T(8,128)S(1)}, s32[8,1024]{1,0:T(8,128)}, u32[]{:S(2)}) copy-start(s32[8,1024]{1,0:T(8,128)} %param.14) | copy-start | bytes 98308
  43.5 13.5 %copy-start.6 = (f32[36,32]{0,1:T(8,128)S(1)}, f32[36,32]{0,1:T(8,128)}, u32[]{:S(2)}) copy-start(f32[36,32]{0,1:T(8,128)} %param.13) | copy-start | bytes 13828
  43.5 28.3 %copy-start.5 = (f32[8,1024]{1,0:T(8,128)S(1)}, f32[8,1024]{1,0:T(8,128)}, u32[]{:S(2)}) copy-start(f32[8,1024]{1,0:T(8,128)} %param.15) | copy-start | bytes 98308
  43.5 64.2 %copy-start.4 = (f32[8,1024]{1,0:T(8,128)S(1)}, f32[8,1024]{1,0:T(8,128)}, u32[]{:S(2)}) copy-start(f32[8,1024]{1,0:T(8,128)} %param.16) | copy-start | bytes 98308
  108.7 1.4 copy-start.1
  151.9 3.1 %copy-start.2 = (f32[162,1024]{1,0:T(8,128)S(1)}, f32[162,1024]{1,0:T(8,128)}, u32[]{:S(2)}) copy-start(f32[162,1024]{1,0:T(8,128)} %param.10) | copy-start | bytes 1990660
  151.9 3.1 %copy-start.8 = (s32[1024]{0:T(1024)S(1)}, s32[1024]{0:T(1024)}, u32[]{:S(2)}) copy-start(s32[1024]{0:T(1024)} %param.12) | copy-start | bytes 12292
  158.6 47.3 %all-to-all-start.1 = ((f32[162,8,128]{2,0,1:T(8,128)}), f32[162,8,128]{2,0,1:T(8,128)S(1)}, u32[]{:S(2)}, u32[]{:S(2)}) async-start(f32[162,8,128]{2,0,1:T(8,128)} %copy.31), calls=%async_computation.1 | async-start | bytes 1376256 | tf_op jit(solution)/shard_map/all_to_all | solution.py:91
  206.4 22.8 %copy-start.7 = (f32[128]{0:T(128)}, f32[128]{0:T(128)S(1)}, u32[]{:S(2)}) copy-start(f32[128]{0:T(128)S(1)} %get-tuple-element.3) | copy-start | bytes 1540
